TPU v7x, 512 devices: a whole 4x4x16 slice. The times are simulated.
512 devices in a mesh: lon: 16 (over z), lat: 8 (over x, y_lo), ens: 4 (over y_hi, core).
Axes of the slice: x: 4, y: 4 (y_hi: 2, y_lo: 2; y = y_hi * 2 + y_lo), z: 16, core: 2. Of those that a mesh axis runs over, the one named last changes fastest.
Arguments:
- field: bfloat16 [4, 128, 1024, 128], P('ens', 'lat', 'lon'), may hold values from -6 to 6
- cotangent: bfloat16 [4, 128, 1024, 128], P('ens', 'lat', 'lon'), may hold values from -6 to 6
- land_mask: int32 [128, 1024], P('lat', 'lon'), may hold values from 0 to 1, as said below
- kernel_taps: float32 [49, 128], replicated, may hold values from -0.875 to 0.875
- norm_gain: float32 [128], replicated, may hold values from 0.1 to 1.9
- norm_shift: float32 [128], replicated, may hold values from -3 to 3
- up_weight: bfloat16 [128, 256], replicated, may hold values from -0.5 to 0.5
- down_weight: bfloat16 [256, 128], replicated, may hold values from -0.375 to 0.375
Outputs:
- output: bfloat16 [4, 128, 1024, 128], P('ens', 'lat', 'lon')
- field_grad: bfloat16 [4, 128, 1024, 128], P('ens', 'lat', 'lon')
- kernel_grad: float32 [49, 128], replicated
- norm_grad: float32 [2, 128], replicated
- up_grad: float32 [128, 256], replicated
- down_grad: float32 [256, 128], replicated
Inputs may be any that keep to these rules, and one draw needn't show every extreme that they name: `land_mask`: 1 marks an ocean cell and 0 a land cell; the share of ocean differs from tile to tile.
All inputs are finite; a program needn't handle non-finite values.
Results may differ from a plain program's by a relative error of at most 0.0062.
Values may be sent and summed in bfloat16 or wider, within the bound.
A program may use at most 64 MiB of HBM per device.

v0:
```python
import math
import jax
import jax.numpy as jnp
from jax import lax
from jax.sharding import PartitionSpec as P

KERNEL = 7
DILATION = 2
REACH = 6


def partner(shard, axis, bit):
    return lax.ppermute(shard, axis, [(i, i ^ 1 << bit) for i in range(lax.axis_size(axis))])


def extended_2(cells, sides, width, closed):
    for axis, dim in sides:
        count = lax.axis_size(axis)
        ends = count if closed else count - 1
        head = lax.slice_in_dim(cells, 0, width, axis=dim)
        tail = lax.slice_in_dim(cells, cells.shape[dim] - width, cells.shape[dim], axis=dim)
        cells = jnp.concatenate(
            [
                lax.ppermute(tail, axis, [(i, (i + 1) % count) for i in range(ends)]),
                cells,
                lax.ppermute(head, axis, [((i + 1) % count, i) for i in range(ends)]),
            ],
            axis=dim,
        )
    return cells


def shifted(block, axis, distance):
    devices = range(lax.axis_size(axis))
    route = [((i - distance) % len(devices), i) for i in devices]
    return lax.ppermute(block, axis, route)


def passed_along(value, axis, steps):
    count = lax.axis_size(axis)
    leading, last = (max(0, -steps), min(count, count - steps))
    return lax.ppermute(value, axis, [(source, source + steps) for source in range(leading, last)])


def depthwise(widened, kernel_taps, rows, cols):
    total = jnp.zeros((rows, cols, widened.shape[2]), jnp.float32)
    for row_tap in range(KERNEL):
        for col_tap in range(KERNEL):
            window = widened[
                DILATION * row_tap : DILATION * row_tap + rows,
                DILATION * col_tap : DILATION * col_tap + cols,
            ]
            total = total + kernel_taps[row_tap * KERNEL + col_tap] * window
    return total


def fold_forward(strip):
    for bit_pos in range(lax.axis_size("lon").bit_length() - 1):
        strip = partner(strip, "lon", bit_pos)
    return strip


def fold_backward(strip):
    for bit_pos in range(lax.axis_size("lon").bit_length() - 1):
        strip = partner(strip.astype(jnp.bfloat16), "lon", bit_pos).astype(strip.dtype)
    return strip


def is_northern():
    return lax.axis_index("lat") == lax.axis_size("lat") - 1


def extend_rows(block):
    padded = extended_2(block, (("lat", 0),), REACH, False)
    height = block.shape[0]
    folded = fold_forward(block[height - REACH :][::-1, ::-1])
    upper = jnp.where(is_northern(), folded, padded[height + REACH :])
    return jnp.concatenate([padded[: height + REACH], upper], 0)


def extend_cols(block):
    return extended_2(block, (("lon", 1),), REACH, True)


def retract_cols(grads):
    width = grads.shape[1] - 2 * REACH
    own = grads[:, REACH : REACH + width]
    from_east = shifted(grads[:, :REACH].astype(jnp.bfloat16), "lon", -1).astype(jnp.float32)
    from_west = shifted(grads[:, REACH + width :].astype(jnp.bfloat16), "lon", 1).astype(
        jnp.float32
    )
    own = own.at[:, width - REACH :].add(from_east)
    return own.at[:, :REACH].add(from_west)


def retract_rows(grads):
    height = grads.shape[0] - 2 * REACH
    own = grads[REACH : REACH + height]
    upper = grads[REACH + height :]
    from_north = passed_along(grads[:REACH].astype(jnp.bfloat16), "lat", -1).astype(jnp.float32)
    from_south = passed_along(upper.astype(jnp.bfloat16), "lat", 1).astype(upper.dtype)
    folded = fold_backward(upper[::-1, ::-1])
    own = own.at[height - REACH :].add(from_north + jnp.where(is_northern(), folded, 0.0))
    return own.at[:REACH].add(from_south)


def shards(field, cotangent, land_mask, kernel_taps, norm_gain, norm_shift, up_weight, down_weight):
    state = field[0]
    upstream_in = cotangent[0]
    rows, cols, channels = state.shape
    sea = land_mask.astype(jnp.float32)[:, :, None]
    masked = (state.astype(jnp.float32) * sea).astype(jnp.bfloat16)
    extended = extend_cols(extend_rows(masked))
    widened = extended.astype(jnp.float32)
    mixed = depthwise(widened, kernel_taps, rows, cols)
    centered = mixed - jnp.mean(mixed, -1, keepdims=True)
    rstd = lax.rsqrt(jnp.mean(centered * centered, -1, keepdims=True) + 1e-06)
    unit = centered * rstd
    normed = (unit * norm_gain + norm_shift).astype(jnp.bfloat16)
    cells = rows * cols
    flat_norm = normed.reshape(cells, channels)
    pre = jnp.dot(flat_norm, up_weight, preferred_element_type=jnp.float32)
    slope = math.sqrt(2.0 / math.pi)
    tanh_val = jnp.tanh(slope * (pre + 0.044715 * pre * pre * pre))
    activated = (0.5 * pre * (1.0 + tanh_val)).astype(jnp.bfloat16)
    product = jnp.dot(activated, down_weight, preferred_element_type=jnp.float32).reshape(
        rows, cols, channels
    )
    output = ((state.astype(jnp.float32) + product) * sea).astype(jnp.bfloat16)
    upstream = (upstream_in.astype(jnp.float32) * sea).astype(jnp.bfloat16)
    flat_up = upstream.reshape(cells, channels)
    down_part = jnp.dot(activated.T, flat_up, preferred_element_type=jnp.float32)
    act_grad = jnp.dot(flat_up, down_weight.T, preferred_element_type=jnp.float32)
    deriv = 0.5 * (1.0 + tanh_val) + 0.5 * pre * (1.0 - tanh_val * tanh_val) * slope * (
        1.0 + 3.0 * 0.044715 * pre * pre
    )
    pre_grad = (act_grad * deriv).astype(jnp.bfloat16)
    up_part = jnp.dot(flat_norm.T, pre_grad, preferred_element_type=jnp.float32)
    norm_in_grad = jnp.dot(pre_grad, up_weight.T, preferred_element_type=jnp.float32).reshape(
        rows, cols, channels
    )
    norm_part = jnp.stack([jnp.sum(norm_in_grad * unit, (0, 1)), jnp.sum(norm_in_grad, (0, 1))])
    count = cells * lax.axis_size("lon") * lax.axis_size("lat") * lax.axis_size("ens")
    factor = 1.0 / math.sqrt(count)
    scaled = norm_in_grad * norm_gain
    mixed_grad = rstd * (
        scaled
        - jnp.mean(scaled, -1, keepdims=True)
        - unit * jnp.mean(scaled * unit, -1, keepdims=True)
    )
    kernel_rows = []
    for row_tap in range(KERNEL):
        for col_tap in range(KERNEL):
            window = widened[
                DILATION * row_tap : DILATION * row_tap + rows,
                DILATION * col_tap : DILATION * col_tap + cols,
            ]
            kernel_rows.append(jnp.sum(window * mixed_grad, (0, 1)))
    kernel_part = jnp.stack(kernel_rows)
    margin = 2 * REACH
    spread_grad = jnp.pad(mixed_grad, ((margin, margin), (margin, margin), (0, 0)))
    extended_grad = jnp.zeros((rows + margin, cols + margin, channels), jnp.float32)
    for row_tap in range(KERNEL):
        for col_tap in range(KERNEL):
            row_start = margin - DILATION * row_tap
            col_start = margin - DILATION * col_tap
            window = spread_grad[
                row_start : row_start + rows + margin, col_start : col_start + cols + margin
            ]
            extended_grad = extended_grad + kernel_taps[row_tap * KERNEL + col_tap] * window
    masked_grad = retract_rows(retract_cols(extended_grad))
    field_grad = ((upstream_in.astype(jnp.float32) + masked_grad) * sea).astype(jnp.bfloat16)
    kernel_sum, norm_sum, up_sum, down_sum = lax.psum(
        (kernel_part, norm_part, up_part, down_part), ("lon", "lat", "ens")
    )
    return (
        output[None],
        field_grad[None],
        kernel_sum * factor,
        norm_sum * factor,
        up_sum * factor,
        down_sum * factor,
    )


def solution(mesh):
    in_specs = (
        P("ens", "lat", "lon", None),
        P("ens", "lat", "lon", None),
        P("lat", "lon"),
        P(),
        P(),
        P(),
        P(),
        P(),
    )
    out_specs = (P("ens", "lat", "lon", None), P("ens", "lat", "lon", None), P(), P(), P(), P())
    return jax.shard_map(shards, mesh=mesh, in_specs=in_specs, out_specs=out_specs, check_vma=False)
```

profile of v0, /device:TPU:36, one launch (start us, length us, event | category | flops | bytes accessed | tf_op | source)
XLA Modules:
  0.0 698.0 jit_solution(13167900297526407773)
XLA Ops:
  7.2 0.0 copy-start
  7.2 0.0 copy-start.2
  7.2 0.0 all-reduce.5.cloned.1.call-start
  7.3 0.8 convert_element_type.87
  8.0 1.1 fusion.106
  9.2 2.0 collective-permute-start.1
  11.3 3.5 collective-permute-start
  14.7 3.3 collective-permute-start.5
  18.0 0.1 mul.1350
  18.1 0.0 collective-permute-done.1
  18.1 5.2 collective-permute-start.2
  23.3 0.2 fusion.107
  23.5 2.4 collective-permute-done.2
  25.9 9.1 %collective-permute-start.3 = (bf16[6,64,128]{2,1,0:T(8,128)(2,1)S(1)}, bf16[6,64,128]{2,1,0:T(8,128)(2,1)S(1)}, u32[]{:S(2)}, u32[]{:S(2)}) collective-permute-start(bf16[6,64,128]{2,1,0:T(8,128)(2,1)S(1)} %collective-permute-done.2), channel_id=1, source_target_pairs={{0,128},{32,160},{64,192},{96,224},{128,0},{160,32},{192,64},{224,... | collective-permute-start | bytes 294920 | tf_op jit(solution)/shard_map/ppermute | solution.py:13
  35.0 4.4 collective-permute-done.3
  39.4 14.6 %collective-permute-start.4 = (bf16[6,64,128]{2,1,0:T(8,128)(2,1)S(1)}, bf16[6,64,128]{2,1,0:T(8,128)(2,1)S(1)}, u32[]{:S(2)}, u32[]{:S(2)}) collective-permute-start(bf16[6,64,128]{2,1,0:T(8,128)(2,1)S(1)} %collective-permute-done.3), channel_id=1, source_target_pairs={{0,256},{32,288},{64,320},{96,352},{128,384},{160,416},{192,448},{... | collective-permute-start | bytes 294920 | tf_op jit(solution)/shard_map/ppermute | solution.py:13
  54.1 0.0 collective-permute-done.5
  54.1 5.7 collective-permute-done.4
  59.8 1.9 collective-permute-start.6
  61.8 3.9 collective-permute-start.7
  65.7 0.2 collective-permute-done.6
  65.9 1.9 collective-permute-done.7
  67.8 0.2 maximum_convert_fusion
  68.0 0.0 copy-start.6
  68.0 0.0 copy-start.7
  68.1 3.9 fusion.116
  72.0 0.4 multiply_reduce_fusion.52
  72.4 0.3 add_convert_fusion
  72.8 0.0 copy-start.4
  72.8 0.5 multiply_convert_fusion
  73.3 1.0 fusion.122
  74.3 0.3 fusion.120
  74.6 0.8 fusion
  75.4 0.9 fusion.121
  76.3 0.4 fusion.113
  76.7 0.1 div.17
  76.8 0.5 multiply_reduce_fusion
  77.3 1.5 multiply_reduce_fusion.1
  78.8 0.7 multiply_reduce_fusion.37
  79.5 0.9 multiply_reduce_fusion.19
  80.4 10.4 %fusion.114 = (bf16[28,76,128]{2,1,0:T(8,128)(2,1)S(1)}, f32[28,76,128]{2,1,0:T(8,128)S(1)}) fusion(f32[128]{0:T(128)S(1)} %get-tuple-element.172, f32[128]{0:T(128)S(1)} %get-tuple-element.173, f32[128]{0:T(128)S(1)} %get-tuple-element.126, f32[128]{0:T(128)S(1)} %get-tuple-element.127, f32[128]{0:T(128)S(1)} %get-tuple-element.128, ...), kind=kLoop, calls=%fused_computation.297 | loop fusion | flops 26693632 | bytes 2183680 | tf_op jit(solution)/shard_map/convert.5
  90.8 0.9 fusion.104
  91.8 2.8 collective-permute-start.9
  94.5 5.5 collective-permute-start.8
  100.1 0.1 slice.883
  100.2 0.1 stack.208
  100.3 102.3 %all-reduce.1 = (f32[49,128]{1,0:T(8,128)S(1)}, f32[2,128]{1,0:T(2,128)S(1)}) all-reduce(f32[49,128]{1,0:T(8,128)S(1)} %stack.208, f32[2,128]{1,0:T(2,128)S(1)} %pad_maximum_fusion.3), channel_id=1, replica_groups=mesh['lon'=16,'lat'=8,'ens'=4] {'lon','lat','ens'}, use_global_device_ids=true, to_apply=%region_53.54 | all-reduce | flops 6528 | bytes 52224 | tf_op jit(solution)/shard_map/psum | solution.py:173
  202.7 0.2 scatter-add.14
  202.9 0.2 scatter-add.15
  203.3 2.8 collective-permute-start.11
  206.0 0.6 broadcast_multiply_fusion.2
  206.6 0.0 all-reduce.5.cloned.1.call-update
  206.7 3.1 collective-permute-done.11
  209.8 3.5 collective-permute-start.12
  213.3 0.6 broadcast_multiply_fusion.6
  213.9 2.8 collective-permute-start.15
  216.7 4.1 collective-permute-start.10
  220.8 6.5 collective-permute-start.13
  227.3 440.4 %all-reduce.5.cloned.1.call-done = (f32[128,256]{1,0:T(8,128)}, f32[256,128]{1,0:T(8,128)}) async-done(((f32[128,256]{1,0:T(8,128)}, f32[256,128]{1,0:T(8,128)}), (f32[128,256]{1,0:T(8,128)}, f32[256,128]{1,0:T(8,128)})) %all-reduce.5.cloned.1.call-update) | async-done | bytes 262160 | tf_op jit(solution)/shard_map/psum | solution.py:173
  667.7 1.6 broadcast_multiply_fusion.1
  669.3 9.2 %collective-permute-start.14 = (bf16[6,64,128]{2,1,0:T(8,128)(2,1)S(1)}, bf16[6,64,128]{2,1,0:T(8,128)(2,1)S(1)}, u32[]{:S(2)}, u32[]{:S(2)}) collective-permute-start(bf16[6,64,128]{2,1,0:T(8,128)(2,1)S(1)} %collective-permute-done.13), channel_id=1, source_target_pairs={{0,256},{32,288},{64,320},{96,352},{128,384},{160,416},{192,448},{... | collective-permute-start | bytes 294920 | tf_op jit(solution)/shard_map/ppermute | solution.py:13
  678.4 1.6 broadcast_multiply_fusion
  680.0 10.2 %collective-permute-done.14 = bf16[6,64,128]{2,1,0:T(8,128)(2,1)S(1)} collective-permute-done((bf16[6,64,128]{2,1,0:T(8,128)(2,1)S(1)}, bf16[6,64,128]{2,1,0:T(8,128)(2,1)S(1)}, u32[]{:S(2)}, u32[]{:S(2)}) %collective-permute-start.14) | collective-permute-done | bytes 98336 | tf_op jit(solution)/shard_map/ppermute | solution.py:13
  690.3 0.9 fusion.110
  (38 shorter events, 0.5 us)
Async XLA Ops:
  7.2 65.6 %copy-start = (bf16[128,256]{1,0:T(8,128)(2,1)S(1)}, bf16[128,256]{1,0:T(8,128)(2,1)}, u32[]{:S(2)}) copy-start(bf16[128,256]{1,0:T(8,128)(2,1)} %param.22) | copy-start | bytes 196612
  7.2 16.1 %copy-start.2 = (bf16[1,16,64,128]{3,2,1,0:T(8,128)(2,1)S(1)}, bf16[1,16,64,128]{3,2,1,0:T(8,128)(2,1)}, u32[]{:S(2)}) copy-start(bf16[1,16,64,128]{3,2,1,0:T(8,128)(2,1)} %param.17) | copy-start | bytes 786436
  7.2 27.8 %copy-start.5 = (f32[49,128]{1,0:T(8,128)S(1)}, f32[49,128]{1,0:T(8,128)}, u32[]{:S(2)}) copy-start(f32[49,128]{1,0:T(8,128)} %param.19) | copy-start | bytes 75268
  7.2 660.5 %all-reduce.5.cloned.1.call-start = ((), (), s32[]{:S(2)}) async-start(), calls=%async_computation | async-start | bytes 524288 | tf_op jit(solution)/shard_map/psum | solution.py:173
  9.2 8.9 %collective-permute-start.1 = (bf16[6,64,128]{2,1,0:T(8,128)(2,1)S(1)}, bf16[6,64,128]{2,1,0:T(8,128)(2,1)S(1)}, u32[]{:S(2)}, u32[]{:S(2)}) collective-permute-start(bf16[6,64,128]{2,1,0:T(8,128)(2,1)S(1)} %rev.6), channel_id=1, source_target_pairs={{0,32},{32,0},{64,96},{96,64},{128,160},{160,128},{192,224},{224,1... | collective-permute-start | bytes 294920 | tf_op jit(solution)/shard_map/ppermute | solution.py:13
  11.3 48.5 %collective-permute-start = (bf16[6,64,128]{2,1,0:T(8,128)(2,1)S(1)}, bf16[6,64,128]{2,1,0:T(8,128)(2,1)S(1)}, u32[]{:S(2)}, u32[]{:S(2)}) collective-permute-start(bf16[6,64,128]{2,1,0:T(8,128)(2,1)S(1)} %get-tuple-element.124), channel_id=1, source_target_pairs={{0,4},{4,8},{8,12},{12,16},{16,20},{20,24},{24,28},{1,5},{5,9},{9,... | collective-permute-start | bytes 294920 | tf_op jit(solution)/shard_map/ppermute | solution.py:24
  14.7 39.3 %collective-permute-start.5 = (bf16[6,64,128]{2,1,0:T(8,128)(2,1)S(1)}, bf16[6,64,128]{2,1,0:T(8,128)(2,1)S(1)}, u32[]{:S(2)}, u32[]{:S(2)}) collective-permute-start(bf16[6,64,128]{2,1,0:T(8,128)(2,1)S(1)} %get-tuple-element.123), channel_id=1, source_target_pairs={{4,0},{8,4},{12,8},{16,12},{20,16},{24,20},{28,24},{5,1},{9,5},{13... | collective-permute-start | bytes 294920 | tf_op jit(solution)/shard_map/ppermute | solution.py:26
  18.1 7.8 %collective-permute-start.2 = (bf16[6,64,128]{2,1,0:T(8,128)(2,1)S(1)}, bf16[6,64,128]{2,1,0:T(8,128)(2,1)S(1)}, u32[]{:S(2)}, u32[]{:S(2)}) collective-permute-start(bf16[6,64,128]{2,1,0:T(8,128)(2,1)S(1)} %collective-permute-done.1), channel_id=1, source_target_pairs={{0,64},{32,96},{64,0},{96,32},{128,192},{160,224},{192,128},{224,1... | collective-permute-start | bytes 294920 | tf_op jit(solution)/shard_map/ppermute | solution.py:13
  25.9 13.5 %collective-permute-start.3 = (bf16[6,64,128]{2,1,0:T(8,128)(2,1)S(1)}, bf16[6,64,128]{2,1,0:T(8,128)(2,1)S(1)}, u32[]{:S(2)}, u32[]{:S(2)}) collective-permute-start(bf16[6,64,128]{2,1,0:T(8,128)(2,1)S(1)} %collective-permute-done.2), channel_id=1, source_target_pairs={{0,128},{32,160},{64,192},{96,224},{128,0},{160,32},{192,64},{224,... | collective-permute-start | bytes 294920 | tf_op jit(solution)/shard_map/ppermute | solution.py:13
  39.4 20.4 %collective-permute-start.4 = (bf16[6,64,128]{2,1,0:T(8,128)(2,1)S(1)}, bf16[6,64,128]{2,1,0:T(8,128)(2,1)S(1)}, u32[]{:S(2)}, u32[]{:S(2)}) collective-permute-start(bf16[6,64,128]{2,1,0:T(8,128)(2,1)S(1)} %collective-permute-done.3), channel_id=1, source_target_pairs={{0,256},{32,288},{64,320},{96,352},{128,384},{160,416},{192,448},{... | collective-permute-start | bytes 294920 | tf_op jit(solution)/shard_map/ppermute | solution.py:13
  59.8 6.1 collective-permute-start.6
  61.8 6.1 collective-permute-start.7
  68.0 4.4 copy-start.6
  68.0 4.4 copy-start.7
  72.8 1.5 copy-start.4
  80.4 10.5 %copy-start.1 = (bf16[1,16,64,128]{3,2,1,0:T(8,128)(2,1)S(1)}, bf16[1,16,64,128]{3,2,1,0:T(8,128)(2,1)}, u32[]{:S(2)}) copy-start(bf16[1,16,64,128]{3,2,1,0:T(8,128)(2,1)} %param.16) | copy-start | bytes 786436
  91.8 111.2 %collective-permute-start.9 = (bf16[28,6,128]{2,1,0:T(8,128)(2,1)S(1)}, bf16[28,6,128]{2,1,0:T(8,128)(2,1)S(1)}, u32[]{:S(2)}, u32[]{:S(2)}) collective-permute-start(bf16[28,6,128]{2,1,0:T(8,128)(2,1)S(1)} %get-tuple-element.119), channel_id=1, source_target_pairs={{480,0},{0,32},{32,64},{64,96},{96,128},{128,160},{160,192},{192,2... | collective-permute-start | bytes 129032 | tf_op jit(solution)/shard_map/ppermute | solution.py:36
  94.5 108.1 %collective-permute-start.8 = (bf16[28,6,128]{2,1,0:T(8,128)(2,1)S(1)}, bf16[28,6,128]{2,1,0:T(8,128)(2,1)S(1)}, u32[]{:S(2)}, u32[]{:S(2)}) collective-permute-start(bf16[28,6,128]{2,1,0:T(8,128)(2,1)S(1)} %get-tuple-element.120), channel_id=1, source_target_pairs={{32,0},{64,32},{96,64},{128,96},{160,128},{192,160},{224,192},{256... | collective-permute-start | bytes 129032 | tf_op jit(solution)/shard_map/ppermute | solution.py:36
  203.3 6.5 collective-permute-start.11
  209.8 11.0 %collective-permute-start.12 = (bf16[6,64,128]{2,1,0:T(8,128)(2,1)S(1)}, bf16[6,64,128]{2,1,0:T(8,128)(2,1)S(1)}, u32[]{:S(2)}, u32[]{:S(2)}) collective-permute-start(bf16[6,64,128]{2,1,0:T(8,128)(2,1)S(1)} %collective-permute-done.11), channel_id=1, source_target_pairs={{0,64},{32,96},{64,0},{96,32},{128,192},{160,224},{192,128},{224,1... | collective-permute-start | bytes 294920 | tf_op jit(solution)/shard_map/ppermute | solution.py:13
  213.8 476.4 %copy-start.3 = (bf16[1,16,64,128]{3,2,1,0:T(8,128)(2,1)S(1)}, bf16[1,16,64,128]{3,2,1,0:T(8,128)(2,1)}, u32[]{:S(2)}) copy-start(bf16[1,16,64,128]{3,2,1,0:T(8,128)(2,1)} %param.17) | copy-start | bytes 786436
  213.9 476.3 %collective-permute-start.15 = (bf16[6,64,128]{2,1,0:T(8,128)(2,1)S(1)}, bf16[6,64,128]{2,1,0:T(8,128)(2,1)S(1)}, u32[]{:S(2)}, u32[]{:S(2)}) collective-permute-start(bf16[6,64,128]{2,1,0:T(8,128)(2,1)S(1)} %get-tuple-element.116), channel_id=1, source_target_pairs={{0,4},{4,8},{8,12},{12,16},{16,20},{20,24},{24,28},{1,5},{5,9},{9,... | collective-permute-start | bytes 294920 | tf_op jit(solution)/shard_map/ppermute | solution.py:42
  216.7 463.3 %collective-permute-start.10 = (bf16[6,64,128]{2,1,0:T(8,128)(2,1)S(1)}, bf16[6,64,128]{2,1,0:T(8,128)(2,1)S(1)}, u32[]{:S(2)}, u32[]{:S(2)}) collective-permute-start(bf16[6,64,128]{2,1,0:T(8,128)(2,1)S(1)} %get-tuple-element.118), channel_id=1, source_target_pairs={{4,0},{8,4},{12,8},{16,12},{20,16},{24,20},{28,24},{5,1},{9,5},{13... | collective-permute-start | bytes 294920 | tf_op jit(solution)/shard_map/ppermute | solution.py:42
  220.8 448.5 %collective-permute-start.13 = (bf16[6,64,128]{2,1,0:T(8,128)(2,1)S(1)}, bf16[6,64,128]{2,1,0:T(8,128)(2,1)S(1)}, u32[]{:S(2)}, u32[]{:S(2)}) collective-permute-start(bf16[6,64,128]{2,1,0:T(8,128)(2,1)S(1)} %collective-permute-done.12), channel_id=1, source_target_pairs={{0,128},{32,160},{64,192},{96,224},{128,0},{160,32},{192,64},{224,... | collective-permute-start | bytes 294920 | tf_op jit(solution)/shard_map/ppermute | solution.py:13
  669.3 20.9 %collective-permute-start.14 = (bf16[6,64,128]{2,1,0:T(8,128)(2,1)S(1)}, bf16[6,64,128]{2,1,0:T(8,128)(2,1)S(1)}, u32[]{:S(2)}, u32[]{:S(2)}) collective-permute-start(bf16[6,64,128]{2,1,0:T(8,128)(2,1)S(1)} %collective-permute-done.13), channel_id=1, source_target_pairs={{0,256},{32,288},{64,320},{96,352},{128,384},{160,416},{192,448},{... | collective-permute-start | bytes 294920 | tf_op jit(solution)/shard_map/ppermute | solution.py:13
Sparse Core Ops, SparseCore 0:
  206.8 460.8 all-reduce.4
where the time goes:
time: 699 us; the launch traced here: 698 us
  waiting for transfers between devices  468 us (67%)
  blocking collectives  102 us (15%)
  starting transfers between devices  80.6 us (12%)
  other arithmetic  27.3 us (4%)
  between operations  14.5 us (2%)
    psum x1, waiting for transfers between devices, shards(): lax.psum((kernel_part, norm_part, up_part, down_part), ('lon', 'lat', 'en...  440 us
    psum x1, blocking collectives, shards(): lax.psum((kernel_part, norm_part, up_part, down_part), ('lon', 'lat', 'en...  102 us
    ppermute x8, starting transfers between devices, partner(): lax.ppermute(shard, axis, [(i, i ^ 1 << bit) for i in range(lax.axis_size...  52.8 us
    ppermute x8, waiting for transfers between devices, partner(): lax.ppermute(shard, axis, [(i, i ^ 1 << bit) for i in range(lax.axis_size...  25.8 us
  transfers between devices with their start and end apart: 17, of which 8 were waited for; matrix products, arithmetic and copies ran while one was open for 1% of the time, Pallas kernels for 0%

commit v1 on v0

--- a/solution.py
+++ b/solution.py
@@ -171,7 +171,7 @@
     masked_grad = retract_rows(retract_cols(extended_grad))
     field_grad = ((upstream_in.astype(jnp.float32) + masked_grad) * sea).astype(jnp.bfloat16)
     kernel_sum, norm_sum, up_sum, down_sum = lax.psum(
-        (kernel_part, norm_part, up_part, down_part), ("lon", "lat", "ens")
+        lax.psum((kernel_part, norm_part, up_part, down_part), ("lat", "ens")), "lon"
     )
     return (
         output[None],

time: 699 us -> 435 us (0.62)
  the two profiles are of different devices: /device:TPU:36 before, /device:TPU:2 now
where the time goes in v1:
time: 435 us
  blocking collectives  162 us (37%)
  waiting for transfers between devices  136 us (31%)
  starting transfers between devices  85 us (20%)
  other arithmetic  29.3 us (7%)
  between operations  15.2 us (3%)
    psum x1, waiting for transfers between devices, shards(): lax.psum(lax.psum((kernel_part, norm_part, up_part, down_part), ('lat', '...  112 us
    psum x1, blocking collectives, shards(): lax.psum((kernel_part, norm_part, up_part, down_part), ('lat', 'ens'))  108 us
    psum x1, blocking collectives, shards(): lax.psum(lax.psum((kernel_part, norm_part, up_part, down_part), ('lat', '...  54.4 us
    ppermute x8, starting transfers between devices, partner(): lax.ppermute(shard, axis, [(i, i ^ 1 << bit) for i in range(lax.axis_size...  49.8 us
    ppermute x8, waiting for transfers between devices, partner(): lax.ppermute(shard, axis, [(i, i ^ 1 << bit) for i in range(lax.axis_size...  19.3 us
    ppermute x2, starting transfers between devices, passed_along(): lax.ppermute(value, axis, [(source, source + steps) for source in range(l...  12.2 us
    another operation x1, other arithmetic  10.3 us
    ppermute x2, starting transfers between devices, extended_2(): lax.ppermute(head, axis, [((i + 1) % count, i) for i in range(ends)])  9.82 us
  transfers between devices with their start and end apart: 18, of which 8 were waited for; matrix products, arithmetic and copies ran while one was open for 2% of the time, Pallas kernels for 0%

profile of v1, /device:TPU:2, one launch (start us, length us, event | category | flops | bytes accessed | tf_op | source)
XLA Modules:
  0.0 434.8 jit_solution(13616564204562798023)
XLA Ops:
  7.2 0.0 copy-start
  7.2 0.0 copy-start.4
  7.2 0.0 all-reduce.8.cloned.1.call-start
  7.2 0.8 convert_element_type.87
  8.0 1.1 fusion.106
  9.2 3.8 collective-permute-start.1
  13.1 3.5 collective-permute-start
  16.6 3.3 collective-permute-start.5
  19.8 0.1 mul.1350
  19.9 5.2 %collective-permute-start.2 = (bf16[6,64,128]{2,1,0:T(8,128)(2,1)S(1)}, bf16[6,64,128]{2,1,0:T(8,128)(2,1)S(1)}, u32[]{:S(2)}, u32[]{:S(2)}) collective-permute-start(bf16[6,64,128]{2,1,0:T(8,128)(2,1)S(1)} %collective-permute-done.1), channel_id=1, source_target_pairs={{0,64},{32,96},{64,0},{96,32},{128,192},{160,224},{192,128},{224,1... | collective-permute-start | bytes 294920 | tf_op jit(solution)/shard_map/ppermute | solution.py:13
  25.1 0.2 fusion.107
  25.3 3.6 collective-permute-done.2
  28.8 9.1 %collective-permute-start.3 = (bf16[6,64,128]{2,1,0:T(8,128)(2,1)S(1)}, bf16[6,64,128]{2,1,0:T(8,128)(2,1)S(1)}, u32[]{:S(2)}, u32[]{:S(2)}) collective-permute-start(bf16[6,64,128]{2,1,0:T(8,128)(2,1)S(1)} %collective-permute-done.2), channel_id=1, source_target_pairs={{0,128},{32,160},{64,192},{96,224},{128,0},{160,32},{192,64},{224,... | collective-permute-start | bytes 294920 | tf_op jit(solution)/shard_map/ppermute | solution.py:13
  38.0 6.9 %collective-permute-done.3 = bf16[6,64,128]{2,1,0:T(8,128)(2,1)S(1)} collective-permute-done((bf16[6,64,128]{2,1,0:T(8,128)(2,1)S(1)}, bf16[6,64,128]{2,1,0:T(8,128)(2,1)S(1)}, u32[]{:S(2)}, u32[]{:S(2)}) %collective-permute-start.3) | collective-permute-done | bytes 98336 | tf_op jit(solution)/shard_map/ppermute | solution.py:13
  44.9 12.4 %collective-permute-start.4 = (bf16[6,64,128]{2,1,0:T(8,128)(2,1)S(1)}, bf16[6,64,128]{2,1,0:T(8,128)(2,1)S(1)}, u32[]{:S(2)}, u32[]{:S(2)}) collective-permute-start(bf16[6,64,128]{2,1,0:T(8,128)(2,1)S(1)} %collective-permute-done.3), channel_id=1, source_target_pairs={{0,256},{32,288},{64,320},{96,352},{128,384},{160,416},{192,448},{... | collective-permute-start | bytes 294920 | tf_op jit(solution)/shard_map/ppermute | solution.py:13
  57.4 4.2 collective-permute-done.4
  61.6 2.1 collective-permute-start.6
  63.7 6.6 %collective-permute-start.7 = (bf16[28,6,128]{2,1,0:T(8,128)(2,1)S(1)}, bf16[28,6,128]{2,1,0:T(8,128)(2,1)S(1)}, u32[]{:S(2)}, u32[]{:S(2)}) collective-permute-start(bf16[28,6,128]{2,1,0:T(8,128)(2,1)S(1)} %get-tuple-element.126), channel_id=1, source_target_pairs={{32,0},{64,32},{96,64},{128,96},{160,128},{192,160},{224,192},{256... | collective-permute-start | bytes 129032 | tf_op jit(solution)/shard_map/ppermute | solution.py:26
  70.3 0.2 collective-permute-done.6
  70.5 1.6 collective-permute-done.7
  72.1 0.2 maximum_convert_fusion
  72.2 0.0 copy-start.50
  72.3 3.9 fusion.116
  76.2 0.4 multiply_reduce_fusion.52
  76.6 0.3 add_convert_fusion
  77.0 0.5 multiply_convert_fusion
  77.5 0.2 copy-done.1
  77.7 1.0 fusion.122
  78.7 0.3 fusion.120
  79.0 0.8 fusion
  79.8 0.4 fusion.113
  80.2 0.1 div.17
  80.3 0.9 multiply_reduce_fusion
  81.1 2.1 multiply_reduce_fusion.1
  83.2 1.2 multiply_reduce_fusion.37
  84.5 1.5 multiply_reduce_fusion.19
  86.0 10.3 %fusion.114 = (bf16[28,76,128]{2,1,0:T(8,128)(2,1)S(1)}, f32[28,76,128]{2,1,0:T(8,128)S(1)}) fusion(f32[128]{0:T(128)S(1)} %get-tuple-element.176, f32[128]{0:T(128)S(1)} %get-tuple-element.177, f32[128]{0:T(128)S(1)} %get-tuple-element.130, f32[128]{0:T(128)S(1)} %get-tuple-element.131, f32[128]{0:T(128)S(1)} %get-tuple-element.132, ...), kind=kLoop, calls=%fused_computation.297 | loop fusion | flops 26693632 | bytes 2183680 | tf_op jit(solution)/shard_map/convert.5
  96.3 0.9 fusion.104
  97.3 5.6 %collective-permute-start.8 = (bf16[28,6,128]{2,1,0:T(8,128)(2,1)S(1)}, bf16[28,6,128]{2,1,0:T(8,128)(2,1)S(1)}, u32[]{:S(2)}, u32[]{:S(2)}) collective-permute-start(bf16[28,6,128]{2,1,0:T(8,128)(2,1)S(1)} %get-tuple-element.124), channel_id=1, source_target_pairs={{32,0},{64,32},{96,64},{128,96},{160,128},{192,160},{224,192},{256... | collective-permute-start | bytes 129032 | tf_op jit(solution)/shard_map/ppermute | solution.py:36
  102.9 0.9 fusion.121
  104.2 1.9 collective-permute-start.9
  106.2 0.1 slice.883
  106.3 0.0 all-reduce.8.cloned.1.call-update
  106.3 0.0 all-reduce.10.cloned.1.call-start
  106.8 1.5 stack.208
  108.3 0.2 scatter-add.14
  108.5 3.1 collective-permute-done.9
  111.6 0.2 scatter-add.15
  111.9 1.9 collective-permute-start.11
  113.8 108.1 %all-reduce.1 = (f32[49,128]{1,0:T(8,128)S(1)}, f32[2,128]{1,0:T(2,128)S(1)}) all-reduce(f32[49,128]{1,0:T(8,128)S(1)} %stack.208, f32[2,128]{1,0:T(2,128)S(1)} %pad_maximum_fusion.3), channel_id=1, replica_groups=mesh['lon'=16,'lat'=8,'ens'=4] {'lat','ens'}, use_global_device_ids=true, to_apply=%region_53.54 | all-reduce | flops 6528 | bytes 52224 | tf_op jit(solution)/shard_map/psum | solution.py:174
  221.9 54.4 %all-reduce.3 = (f32[49,128]{1,0:T(8,128)S(1)}, f32[2,128]{1,0:T(2,128)S(1)}) all-reduce(f32[49,128]{1,0:T(8,128)S(1)} %get-tuple-element.107, f32[2,128]{1,0:T(2,128)S(1)} %get-tuple-element.108), channel_id=1, replica_groups=mesh['lon'=16,'lat'=8,'ens'=4] {'lon'}, use_global_device_ids=true, to_apply=%region_54.55 | all-reduce | flops 6528 | bytes 52224 | tf_op jit(solution)/shard_map/psum | solution.py:173
  276.3 0.0 all-reduce.10.cloned.1.call-update
  276.3 2.1 collective-permute-start.12
  278.4 0.6 broadcast_multiply_fusion.2
  279.0 4.7 %collective-permute-done.12 = bf16[6,64,128]{2,1,0:T(8,128)(2,1)S(1)} collective-permute-done((bf16[6,64,128]{2,1,0:T(8,128)(2,1)S(1)}, bf16[6,64,128]{2,1,0:T(8,128)(2,1)S(1)}, u32[]{:S(2)}, u32[]{:S(2)}) %collective-permute-start.12) | collective-permute-done | bytes 98336 | tf_op jit(solution)/shard_map/ppermute | solution.py:13
  283.7 6.5 %collective-permute-start.13 = (bf16[6,64,128]{2,1,0:T(8,128)(2,1)S(1)}, bf16[6,64,128]{2,1,0:T(8,128)(2,1)S(1)}, u32[]{:S(2)}, u32[]{:S(2)}) collective-permute-start(bf16[6,64,128]{2,1,0:T(8,128)(2,1)S(1)} %collective-permute-done.12), channel_id=1, source_target_pairs={{0,128},{32,160},{64,192},{96,224},{128,0},{160,32},{192,64},{224,... | collective-permute-start | bytes 294920 | tf_op jit(solution)/shard_map/ppermute | solution.py:13
  290.2 0.6 broadcast_multiply_fusion.6
  290.8 2.1 collective-permute-start.15
  292.9 10.1 %collective-permute-start.10 = (bf16[6,64,128]{2,1,0:T(8,128)(2,1)S(1)}, bf16[6,64,128]{2,1,0:T(8,128)(2,1)S(1)}, u32[]{:S(2)}, u32[]{:S(2)}) collective-permute-start(bf16[6,64,128]{2,1,0:T(8,128)(2,1)S(1)} %get-tuple-element.122), channel_id=1, source_target_pairs={{4,0},{8,4},{12,8},{16,12},{20,16},{24,20},{28,24},{5,1},{9,5},{13... | collective-permute-start | bytes 294920 | tf_op jit(solution)/shard_map/ppermute | solution.py:42
  303.0 8.7 %collective-permute-start.14 = (bf16[6,64,128]{2,1,0:T(8,128)(2,1)S(1)}, bf16[6,64,128]{2,1,0:T(8,128)(2,1)S(1)}, u32[]{:S(2)}, u32[]{:S(2)}) collective-permute-start(bf16[6,64,128]{2,1,0:T(8,128)(2,1)S(1)} %collective-permute-done.13), channel_id=1, source_target_pairs={{0,256},{32,288},{64,320},{96,352},{128,384},{160,416},{192,448},{... | collective-permute-start | bytes 294920 | tf_op jit(solution)/shard_map/ppermute | solution.py:13
  311.8 112.0 %all-reduce.10.cloned.1.call-done = (f32[128,256]{1,0:T(8,128)}, f32[256,128]{1,0:T(8,128)}) async-done(((f32[128,256]{1,0:T(8,128)}, f32[256,128]{1,0:T(8,128)}), (f32[128,256]{1,0:T(8,128)}, f32[256,128]{1,0:T(8,128)})) %all-reduce.10.cloned.1.call-update) | async-done | bytes 262160 | tf_op jit(solution)/shard_map/psum | solution.py:173
  423.8 1.6 broadcast_multiply_fusion.1
  425.4 1.6 broadcast_multiply_fusion
  427.1 0.9 fusion.110
  (128 shorter events, 0.7 us)
Async XLA Ops:
  7.2 69.8 %copy-start = (bf16[128,256]{1,0:T(8,128)(2,1)S(1)}, bf16[128,256]{1,0:T(8,128)(2,1)}, u32[]{:S(2)}) copy-start(bf16[128,256]{1,0:T(8,128)(2,1)} %param.22) | copy-start | bytes 196612
  7.2 17.9 %copy-start.4 = (bf16[1,16,64,128]{3,2,1,0:T(8,128)(2,1)S(1)}, bf16[1,16,64,128]{3,2,1,0:T(8,128)(2,1)}, u32[]{:S(2)}) copy-start(bf16[1,16,64,128]{3,2,1,0:T(8,128)(2,1)} %param.17) | copy-start | bytes 786436
  7.2 30.7 %copy-start.7 = (f32[49,128]{1,0:T(8,128)S(1)}, f32[49,128]{1,0:T(8,128)}, u32[]{:S(2)}) copy-start(f32[49,128]{1,0:T(8,128)} %param.19) | copy-start | bytes 75268
  7.2 269.1 %all-reduce.8.cloned.1.call-start = ((), (), s32[]{:S(2)}) async-start(), calls=%async_computation | async-start | bytes 524288 | tf_op jit(solution)/shard_map/psum | solution.py:174
  9.2 10.7 %collective-permute-start.1 = (bf16[6,64,128]{2,1,0:T(8,128)(2,1)S(1)}, bf16[6,64,128]{2,1,0:T(8,128)(2,1)S(1)}, u32[]{:S(2)}, u32[]{:S(2)}) collective-permute-start(bf16[6,64,128]{2,1,0:T(8,128)(2,1)S(1)} %rev.6), channel_id=1, source_target_pairs={{0,32},{32,0},{64,96},{96,64},{128,160},{160,128},{192,224},{224,1... | collective-permute-start | bytes 294920 | tf_op jit(solution)/shard_map/ppermute | solution.py:13
  13.1 48.5 %collective-permute-start = (bf16[6,64,128]{2,1,0:T(8,128)(2,1)S(1)}, bf16[6,64,128]{2,1,0:T(8,128)(2,1)S(1)}, u32[]{:S(2)}, u32[]{:S(2)}) collective-permute-start(bf16[6,64,128]{2,1,0:T(8,128)(2,1)S(1)} %get-tuple-element.128), channel_id=1, source_target_pairs={{0,4},{4,8},{8,12},{12,16},{16,20},{20,24},{24,28},{1,5},{5,9},{9,... | collective-permute-start | bytes 294920 | tf_op jit(solution)/shard_map/ppermute | solution.py:24
  16.6 40.8 %collective-permute-start.5 = (bf16[6,64,128]{2,1,0:T(8,128)(2,1)S(1)}, bf16[6,64,128]{2,1,0:T(8,128)(2,1)S(1)}, u32[]{:S(2)}, u32[]{:S(2)}) collective-permute-start(bf16[6,64,128]{2,1,0:T(8,128)(2,1)S(1)} %get-tuple-element.127), channel_id=1, source_target_pairs={{4,0},{8,4},{12,8},{16,12},{20,16},{24,20},{28,24},{5,1},{9,5},{13... | collective-permute-start | bytes 294920 | tf_op jit(solution)/shard_map/ppermute | solution.py:26
  19.9 9.0 %collective-permute-start.2 = (bf16[6,64,128]{2,1,0:T(8,128)(2,1)S(1)}, bf16[6,64,128]{2,1,0:T(8,128)(2,1)S(1)}, u32[]{:S(2)}, u32[]{:S(2)}) collective-permute-start(bf16[6,64,128]{2,1,0:T(8,128)(2,1)S(1)} %collective-permute-done.1), channel_id=1, source_target_pairs={{0,64},{32,96},{64,0},{96,32},{128,192},{160,224},{192,128},{224,1... | collective-permute-start | bytes 294920 | tf_op jit(solution)/shard_map/ppermute | solution.py:13
  28.8 16.0 %collective-permute-start.3 = (bf16[6,64,128]{2,1,0:T(8,128)(2,1)S(1)}, bf16[6,64,128]{2,1,0:T(8,128)(2,1)S(1)}, u32[]{:S(2)}, u32[]{:S(2)}) collective-permute-start(bf16[6,64,128]{2,1,0:T(8,128)(2,1)S(1)} %collective-permute-done.2), channel_id=1, source_target_pairs={{0,128},{32,160},{64,192},{96,224},{128,0},{160,32},{192,64},{224,... | collective-permute-start | bytes 294920 | tf_op jit(solution)/shard_map/ppermute | solution.py:13
  44.9 16.6 %collective-permute-start.4 = (bf16[6,64,128]{2,1,0:T(8,128)(2,1)S(1)}, bf16[6,64,128]{2,1,0:T(8,128)(2,1)S(1)}, u32[]{:S(2)}, u32[]{:S(2)}) collective-permute-start(bf16[6,64,128]{2,1,0:T(8,128)(2,1)S(1)} %collective-permute-done.3), channel_id=1, source_target_pairs={{0,256},{32,288},{64,320},{96,352},{128,384},{160,416},{192,448},{... | collective-permute-start | bytes 294920 | tf_op jit(solution)/shard_map/ppermute | solution.py:13
  61.6 8.9 %collective-permute-start.6 = (bf16[28,6,128]{2,1,0:T(8,128)(2,1)S(1)}, bf16[28,6,128]{2,1,0:T(8,128)(2,1)S(1)}, u32[]{:S(2)}, u32[]{:S(2)}) collective-permute-start(bf16[28,6,128]{2,1,0:T(8,128)(2,1)S(1)} %get-tuple-element.125), channel_id=1, source_target_pairs={{0,32},{32,64},{64,96},{96,128},{128,160},{160,192},{192,224},{224... | collective-permute-start | bytes 129032 | tf_op jit(solution)/shard_map/ppermute | solution.py:24
  63.7 8.4 %collective-permute-start.7 = (bf16[28,6,128]{2,1,0:T(8,128)(2,1)S(1)}, bf16[28,6,128]{2,1,0:T(8,128)(2,1)S(1)}, u32[]{:S(2)}, u32[]{:S(2)}) collective-permute-start(bf16[28,6,128]{2,1,0:T(8,128)(2,1)S(1)} %get-tuple-element.126), channel_id=1, source_target_pairs={{32,0},{64,32},{96,64},{128,96},{160,128},{192,160},{224,192},{256... | collective-permute-start | bytes 129032 | tf_op jit(solution)/shard_map/ppermute | solution.py:26
  72.2 4.4 %copy-start.8 = (f32[128]{0:T(128)S(1)}, f32[128]{0:T(128)}, u32[]{:S(2)}) copy-start(f32[128]{0:T(128)} %param.20) | copy-start | bytes 1540
  72.2 4.4 %copy-start.50 = (f32[128]{0:T(128)S(1)}, f32[128]{0:T(128)}, u32[]{:S(2)}) copy-start(f32[128]{0:T(128)} %param.21) | copy-start | bytes 1540
  86.0 10.4 %copy-start.3 = (bf16[1,16,64,128]{3,2,1,0:T(8,128)(2,1)S(1)}, bf16[1,16,64,128]{3,2,1,0:T(8,128)(2,1)}, u32[]{:S(2)}) copy-start(bf16[1,16,64,128]{3,2,1,0:T(8,128)(2,1)} %param.16) | copy-start | bytes 786436
  96.3 6.6 %copy-start.2 = (bf16[16,64,128]{2,1,0:T(8,128)(2,1)S(1)}, bf16[16,64,128]{2,1,0:T(8,128)(2,1)}, u32[]{:S(2)}) copy-start(bf16[16,64,128]{2,1,0:T(8,128)(2,1)} %copy-done.1) | copy-start | bytes 786436
  97.3 11.0 %collective-permute-start.8 = (bf16[28,6,128]{2,1,0:T(8,128)(2,1)S(1)}, bf16[28,6,128]{2,1,0:T(8,128)(2,1)S(1)}, u32[]{:S(2)}, u32[]{:S(2)}) collective-permute-start(bf16[28,6,128]{2,1,0:T(8,128)(2,1)S(1)} %get-tuple-element.124), channel_id=1, source_target_pairs={{32,0},{64,32},{96,64},{128,96},{160,128},{192,160},{224,192},{256... | collective-permute-start | bytes 129032 | tf_op jit(solution)/shard_map/ppermute | solution.py:36
  103.9 2.5 copy-start.12
  103.9 2.5 copy-start.13
  103.9 2.5 copy-start.14
  103.9 2.5 copy-start.15
  103.9 2.5 copy-start.16
  103.9 2.5 copy-start.17
  103.9 2.5 copy-start.18
  104.0 2.5 copy-start.19
  104.0 2.5 copy-start.20
  104.0 2.5 copy-start.21
  104.0 2.5 copy-start.22
  104.0 2.5 copy-start.23
  104.0 2.5 copy-start.24
  104.0 2.5 copy-start.25
  104.0 2.5 copy-start.26
  104.0 2.5 copy-start.27
  104.0 2.5 copy-start.28
  104.0 2.5 copy-start.29
  104.1 2.5 copy-start.30
  104.1 2.5 copy-start.31
  104.1 2.5 copy-start.32
  104.1 2.5 copy-start.33
  104.1 2.5 copy-start.34
  104.1 2.5 copy-start.35
  104.1 2.5 copy-start.36
  104.1 2.5 copy-start.37
  104.1 2.5 copy-start.38
  104.2 2.5 copy-start.39
  104.2 2.5 copy-start.40
  104.2 2.5 copy-start.41
  104.2 2.5 copy-start.42
  104.2 2.5 copy-start.43
  104.2 2.5 copy-start.44
  104.2 2.5 copy-start.45
  104.2 2.5 copy-start.46
  104.2 2.5 copy-start.47
  104.2 2.5 copy-start.48
  104.2 7.3 %collective-permute-start.9 = (bf16[28,6,128]{2,1,0:T(8,128)(2,1)S(1)}, bf16[28,6,128]{2,1,0:T(8,128)(2,1)S(1)}, u32[]{:S(2)}, u32[]{:S(2)}) collective-permute-start(bf16[28,6,128]{2,1,0:T(8,128)(2,1)S(1)} %get-tuple-element.123), channel_id=1, source_target_pairs={{480,0},{0,32},{32,64},{64,96},{96,128},{128,160},{160,192},{192,2... | collective-permute-start | bytes 129032 | tf_op jit(solution)/shard_map/ppermute | solution.py:36
  106.3 317.5 %all-reduce.10.cloned.1.call-start = ((), (), s32[]{:S(2)}) async-start(), calls=%async_computation.1 | async-start | bytes 524288 | tf_op jit(solution)/shard_map/psum | solution.py:173
  108.2 5.6 %copy-start.49 = (f32[128]{0:T(128)S(1)}, f32[128]{0:T(128)}, u32[]{:S(2)}) copy-start(f32[128]{0:T(128)} %get-tuple-element.103) | copy-start | bytes 1540
  111.9 164.4 %collective-permute-start.11 = (bf16[6,64,128]{2,1,0:T(8,128)(2,1)S(1)}, bf16[6,64,128]{2,1,0:T(8,128)(2,1)S(1)}, u32[]{:S(2)}, u32[]{:S(2)}) collective-permute-start(bf16[6,64,128]{2,1,0:T(8,128)(2,1)S(1)} %rev.7), channel_id=1, source_target_pairs={{0,32},{32,0},{64,96},{96,64},{128,160},{160,128},{192,224},{224,1... | collective-permute-start | bytes 294920 | tf_op jit(solution)/shard_map/ppermute | solution.py:13
  276.3 7.4 %collective-permute-start.12 = (bf16[6,64,128]{2,1,0:T(8,128)(2,1)S(1)}, bf16[6,64,128]{2,1,0:T(8,128)(2,1)S(1)}, u32[]{:S(2)}, u32[]{:S(2)}) collective-permute-start(bf16[6,64,128]{2,1,0:T(8,128)(2,1)S(1)} %collective-permute-done.11), channel_id=1, source_target_pairs={{0,64},{32,96},{64,0},{96,32},{128,192},{160,224},{192,128},{224,1... | collective-permute-start | bytes 294920 | tf_op jit(solution)/shard_map/ppermute | solution.py:13
  283.7 19.3 %collective-permute-start.13 = (bf16[6,64,128]{2,1,0:T(8,128)(2,1)S(1)}, bf16[6,64,128]{2,1,0:T(8,128)(2,1)S(1)}, u32[]{:S(2)}, u32[]{:S(2)}) collective-permute-start(bf16[6,64,128]{2,1,0:T(8,128)(2,1)S(1)} %collective-permute-done.12), channel_id=1, source_target_pairs={{0,128},{32,160},{64,192},{96,224},{128,0},{160,32},{192,64},{224,... | collective-permute-start | bytes 294920 | tf_op jit(solution)/shard_map/ppermute | solution.py:13
  290.8 136.3 %copy-start.5 = (bf16[1,16,64,128]{3,2,1,0:T(8,128)(2,1)S(1)}, bf16[1,16,64,128]{3,2,1,0:T(8,128)(2,1)}, u32[]{:S(2)}) copy-start(bf16[1,16,64,128]{3,2,1,0:T(8,128)(2,1)} %param.17) | copy-start | bytes 786436
  290.8 136.2 %collective-permute-start.15 = (bf16[6,64,128]{2,1,0:T(8,128)(2,1)S(1)}, bf16[6,64,128]{2,1,0:T(8,128)(2,1)S(1)}, u32[]{:S(2)}, u32[]{:S(2)}) collective-permute-start(bf16[6,64,128]{2,1,0:T(8,128)(2,1)S(1)} %get-tuple-element.120), channel_id=1, source_target_pairs={{0,4},{4,8},{8,12},{12,16},{16,20},{20,24},{24,28},{1,5},{5,9},{9,... | collective-permute-start | bytes 294920 | tf_op jit(solution)/shard_map/ppermute | solution.py:42
  292.9 134.1 %collective-permute-start.10 = (bf16[6,64,128]{2,1,0:T(8,128)(2,1)S(1)}, bf16[6,64,128]{2,1,0:T(8,128)(2,1)S(1)}, u32[]{:S(2)}, u32[]{:S(2)}) collective-permute-start(bf16[6,64,128]{2,1,0:T(8,128)(2,1)S(1)} %get-tuple-element.122), channel_id=1, source_target_pairs={{4,0},{8,4},{12,8},{16,12},{20,16},{24,20},{28,24},{5,1},{9,5},{13... | collective-permute-start | bytes 294920 | tf_op jit(solution)/shard_map/ppermute | solution.py:42
  303.0 123.9 %collective-permute-start.14 = (bf16[6,64,128]{2,1,0:T(8,128)(2,1)S(1)}, bf16[6,64,128]{2,1,0:T(8,128)(2,1)S(1)}, u32[]{:S(2)}, u32[]{:S(2)}) collective-permute-start(bf16[6,64,128]{2,1,0:T(8,128)(2,1)S(1)} %collective-permute-done.13), channel_id=1, source_target_pairs={{0,256},{32,288},{64,320},{96,352},{128,384},{160,416},{192,448},{... | collective-permute-start | bytes 294920 | tf_op jit(solution)/shard_map/ppermute | solution.py:13
  (5 other events, 9.9 us)
Sparse Core Ops, SparseCore 0:
  106.4 131.7 all-reduce.7
  276.4 147.3 all-reduce.9
